TPU v7x, 768 devices: a whole 4x8x12 slice. The times are simulated.
768 devices in a mesh: tm: 24 (over z_lo, x), slab: 32 (over z_hi, y, core).
Axes of the slice: x: 4, y: 8, z: 12 (z_hi: 2, z_lo: 6; z = z_hi * 6 + z_lo), core: 2. Of those that a mesh axis runs over, the one named last changes fastest.
Arguments:
- initial: float32 [24, 16, 256, 16, 128], P('tm', None, 'slab'), may hold values from -6 to 6
- source: float32 [24, 256, 16, 128], P('tm', 'slab'), may hold values from -6 to 6
- decay_rate: float32 [256, 16, 128], P('slab'), may hold values from 0.01 to 0.2
- observed: float32 [24, 16, 256, 16, 128], P('tm', None, 'slab'), may hold values from -6 to 6
- release: int32 [24, 16], replicated, may hold values from 0 to 3
- smooth_taps: float32 [31], replicated, may hold values from 0.02 to 0.08
Outputs:
- source_gradient: float32 [24, 256, 2048], P('tm', None, 'slab')
- decay_gradient: float32 [24, 256, 2048], P('tm', None, 'slab')
All inputs are finite; a program needn't handle non-finite values.
Results may differ from a plain program's by a relative error of at most 0.0003.
Values sent between devices are 32-bit elements; how exact they have to be, the bound alone decides.
No kernel may reach another device: no remote copies, remote signals or barrier semaphores. Data moves between devices by JAX's collectives and lax.ppermute only.
A program may use at most 32 MiB of HBM per device.

v0:
```python
import jax
import jax.numpy as jnp
from jax import lax
from jax.experimental import pallas as pl
from jax.experimental.pallas import tpu as pltpu
from jax.sharding import PartitionSpec as P

STEPS = 4
REACH = STEPS - 1
HALO = STEPS
CHUNKS = (10, 6)

vertical_rate = 0.2
lateral_rate = 0.1


def operator(value, centre):
    upper, lower = (half[1:-1] for half in value)
    row = lax.broadcasted_iota(jnp.int32, upper.shape, 1)
    lane = lax.broadcasted_iota(jnp.int32, upper.shape, 2)
    ny, nx = upper.shape[1:]
    upper_on, lower_on = pltpu.roll(upper, 1, 1), pltpu.roll(lower, 1, 1)
    upper_back, lower_back = pltpu.roll(upper, ny - 1, 1), pltpu.roll(lower, ny - 1, 1)
    sides = (
        jnp.where(row == 0, 0.0, upper_on) + jnp.where(row == ny - 1, lower_back, upper_back),
        jnp.where(row == 0, upper_on, lower_on) + jnp.where(row == ny - 1, 0.0, lower_back),
    )
    out = []
    for whole, middle, rate, side in zip(value, (upper, lower), centre, sides):
        left = jnp.where(lane == 0, 0.0, pltpu.roll(middle, 1, 2))
        right = jnp.where(lane == nx - 1, 0.0, pltpu.roll(middle, nx - 1, 2))
        vertical = whole[2:] + whole[:-2]
        out.append(middle * rate + vertical + (lateral_rate / vertical_rate) * (side + (left + right)))
    return tuple(out)


def inside(value, width, low, high):
    if width == 0:
        return value
    count = value.shape[0]
    return jnp.concatenate(
        [value[:width] * low, value[width : count - width], value[count - width :] * high], axis=0
    )


def padded(value):
    edge = jnp.zeros((2,) + value.shape[1:], value.dtype)
    return jnp.concatenate([edge, value, edge], axis=0)


def plus_middle(total, value):
    cut = (total.shape[0] - value.shape[0]) // 2
    return jnp.concatenate([total[:cut], total[cut:-cut] + value, total[-cut:]], axis=0)


def halves(value):
    cut = value.shape[1] // 2
    return value[:, :cut], value[:, cut:]


def one_channel(release, start, target, centre, field, low, high):
    scale = 1.0 / vertical_rate
    states = [start]
    for k in range(STEPS):
        part = slice(k, centre[0].shape[0] - k)
        value = operator(states[k], tuple(half[part] for half in centre))
        if release == k:
            value = tuple(v + scale ** (k + 1) * f[part] for v, f in zip(value, field))
        states.append(tuple(inside(v, REACH - k, low, high) for v in value))
    adjoint = tuple(s * scale**-STEPS - t for s, t in zip(states[STEPS], target))
    sums = None
    terms = []
    for k in reversed(range(STEPS)):
        if release == k:
            sums = tuple(a * scale ** (k - REACH) for a in adjoint)
        terms.append(tuple(a * s[1:-1] for a, s in zip(adjoint, states[k])))
        if k > 0:
            part = slice(k - 1, centre[0].shape[0] - (k - 1))
            adjoint = operator(
                tuple(padded(a) for a in adjoint), tuple(half[part] for half in centre)
            )
            adjoint = tuple(inside(a, STEPS - k, low, high) for a in adjoint)
    products = []
    for half in range(2):
        total = terms[-1][half]
        for term in reversed(terms[:-1]):
            total = plus_middle(total, term[half])
        products.append(total)
    return sums, products


def chunk_kernel(
    count,
    offset,
    first,
    last,
    scalars,
    middle,
    before,
    after,
    across,
    crossed,
    target,
    centre_in,
    field_in,
    *rest,
):
    if first:
        (*outs, sums, products, centre, field) = rest
    else:
        (sums_in, products_in, *outs, sums, products, centre, field) = rest
    c = pl.program_id(0)
    low = scalars[16].astype(jnp.float32)
    high = scalars[17].astype(jnp.float32)
    from_low = scalars[18].astype(jnp.float32)
    from_high = scalars[19].astype(jnp.float32)

    @pl.when(c == 0)
    def _():
        cut = HALO - REACH
        size = field.shape[0]
        field[...] = field_in[...]
        field[:REACH] += from_low * crossed[0, cut:]
        field[size - REACH :] += from_high * crossed[0, :REACH]
        centre[...] = centre_in[...]
        centre[:REACH] -= (from_low / vertical_rate) * crossed[1, cut:]
        centre[size - REACH :] -= (from_high / vertical_rate) * crossed[1, :REACH]
        if first:
            sums[...] = jnp.zeros_like(sums)
            products[...] = jnp.zeros_like(products)
        else:
            sums[...] = sums_in[...]
            products[...] = products_in[...]

    release = scalars[offset + c]
    rows = sums.shape[1] // 2

    def run(step):
        crossing = across[0]
        start = jnp.concatenate(
            [before[0] + from_low * crossing, middle[0], after[0] + from_high * crossing], axis=0
        )
        totals, found = one_channel(
            step, halves(start), halves(target[0, 0]), halves(centre[...]), halves(field[...]), low, high
        )
        for half, (total, product) in enumerate(zip(totals, found)):
            part = slice(half * rows, (half + 1) * rows)
            reach = slice(step, sums.shape[0] - step)
            sums[reach, part] += total
            products[:, part] -= product

    for k in range(STEPS):
        pl.when(release == k)(lambda k=k: run(k))

    @pl.when(c == count - 1)
    def _():
        if last:
            write_blocks(sums[...], products[...] * vertical_rate**REACH, outs[0])
        else:
            outs[0][...] = sums[...]
            outs[1][...] = products[...]


def write_blocks(first, second, out):
    edge = jnp.zeros((1,) + first.shape[1:], first.dtype)
    first = jnp.concatenate([edge, first, edge], axis=0)
    second = jnp.concatenate([edge, second, edge], axis=0)
    half = first.shape[-1] // 2
    lane = lax.broadcasted_iota(jnp.int32, first.shape, 2)
    even = jnp.where(lane < half, first, pltpu.roll(second, half, 2))
    odd = jnp.where(lane < half, pltpu.roll(first, half, 2), second)
    out[:, 0] = jnp.transpose(even, (1, 0, 2))
    out[:, 1] = jnp.transpose(odd, (1, 0, 2))


def vmem():
    return pl.BlockSpec(memory_space=pltpu.VMEM)


def run_chunk(count, offset, last, scalars, middle, before, after, across, observed, centre, field, carried):
    layers, ny, nx = middle.shape[1:]
    first = not carried
    wide = (layers + 2 * REACH, ny, nx)
    flat = pl.BlockSpec(wide, lambda c: (0, 0, 0))
    if last:
        shapes = (jax.ShapeDtypeStruct((ny, 2, layers + 2 * HALO, nx), jnp.float32),)
        out_specs = (pl.BlockSpec(shapes[0].shape, lambda c: (0, 0, 0, 0)),)
    else:
        shapes = (jax.ShapeDtypeStruct(wide, jnp.float32),) * 2
        out_specs = (flat, flat)

    def kernel(*refs):
        chunk_kernel(count, offset, first, last, *refs)

    return pl.pallas_call(
        kernel,
        grid=(count,),
        out_shape=shapes,
        in_specs=[
            pl.BlockSpec(memory_space=pltpu.SMEM),
            pl.BlockSpec((1, layers, ny, nx), lambda c: (c, 0, 0, 0)),
            pl.BlockSpec((1, HALO, ny, nx), lambda c: (c, before.shape[1] // HALO - 1, 0, 0)),
            pl.BlockSpec((1, HALO, ny, nx), lambda c: (c, 0, 0, 0)),
            pl.BlockSpec((1, HALO, ny, nx), lambda c: (offset + c + 2, 0, 0, 0)),
            pl.BlockSpec((2, HALO, ny, nx), lambda c: (0, 0, 0, 0)),
            pl.BlockSpec((1, 1, layers, ny, nx), lambda c: (0, offset + c, 0, 0, 0)),
            flat,
            flat,
        ]
        + [flat] * len(carried),
        out_specs=out_specs,
        scratch_shapes=[pltpu.VMEM(wide, jnp.float32)] * 4,
        cost_estimate=pl.CostEstimate(
            flops=count * 4000000, bytes_accessed=count * 250000, transcendentals=0
        ),
        name="last_chunk" if last else "chunk",
    )(scalars, middle, before, after, across, across, observed, centre, field, *carried)


def prepare_kernel(taps, source, decay, before, after, centre, field, matrix):
    def spread(mid, slot):
        layers = mid.shape[0]
        return jnp.concatenate(
            [before[slot, layers - REACH :], mid, after[slot, :REACH]], axis=0
        )

    field[...] = spread(source[0], 0)
    rate = 1.0 - 2.0 * vertical_rate - 4.0 * lateral_rate - spread(decay[...], 1)
    centre[...] = rate * (1.0 / vertical_rate)

    depth = matrix.shape[1]
    layers = source.shape[1]
    block = layers + 2 * HALO
    count = taps.shape[0]

    def fill(slab, _):
        shape = (block, depth)
        layer = lax.broadcasted_iota(jnp.int32, shape, 0) + (slab * layers - HALO)
        offset = layer - lax.broadcasted_iota(jnp.int32, shape, 1) + (count - 1) // 2
        offset = jnp.where((layer >= 0) & (layer < depth), offset, -1)
        value = jnp.zeros(shape, jnp.float32)
        for tap in range(count):
            value = jnp.where(offset == tap, taps[tap], value)
        matrix[pl.ds(pl.multiple_of(slab * block, block), block), :] = value
        return 0

    lax.fori_loop(0, matrix.shape[0] // block, fill, 0)


def prepare(slabs, taps, source, decay, before, after):
    layers, ny, nx = decay.shape
    wide = jax.ShapeDtypeStruct((layers + 2 * REACH, ny, nx), jnp.float32)
    matrix = jax.ShapeDtypeStruct((slabs * (layers + 2 * HALO), slabs * layers), jnp.float32)
    smem = pl.BlockSpec(memory_space=pltpu.SMEM)
    return pl.pallas_call(
        prepare_kernel,
        grid=(1,),
        out_shape=(wide, wide, matrix),
        in_specs=[smem]
        + [pl.BlockSpec(a.shape, lambda c, n=a.ndim: (0,) * n) for a in (source, decay, before, after)],
        out_specs=tuple(pl.BlockSpec(a.shape, lambda c, n=len(a.shape): (0,) * n) for a in (wide, wide, matrix)),
        cost_estimate=pl.CostEstimate(flops=8000000, bytes_accessed=2000000, transcendentals=0),
        name="prepare",
    )(taps, source, decay, before, after)


def smooth_kernel(matrix, columns, source_out, decay_out):
    result = lax.dot_general(
        columns[...],
        matrix[...],
        (((0,), (0,)), ((), ())),
        preferred_element_type=jnp.float32,
        precision=lax.Precision.HIGHEST,
    )
    half = result.shape[0] // 2
    source_out[...] = result[:half]
    decay_out[...] = result[half:]


def smooth(matrix, columns):
    depth = matrix.shape[1]
    half = columns.shape[1] // 2
    shape = jax.ShapeDtypeStruct((half, depth), jnp.float32)
    return pl.pallas_call(
        smooth_kernel,
        out_shape=(shape, shape),
        in_specs=[vmem(), vmem()],
        out_specs=(vmem(), vmem()),
        name="smooth",
    )(matrix, columns)


def body(initial, source, decay_rate, observed, release, smooth_taps):
    groups = lax.axis_size("tm")
    slabs = lax.axis_size("slab")
    half_way = groups // 2
    centre_cut = slabs // 2
    tm_index = lax.axis_index("tm")
    slab_index = lax.axis_index("slab")
    own_initial = initial[0]
    layers = own_initial.shape[1]

    across_tm = [(i, (i + half_way) % groups) for i in range(groups)]
    upward = [(s, s + 1) for s in range(slabs - 1) if s != centre_cut - 1]
    downward = [(t, s) for s, t in upward]
    crossing_pairs = []
    for i, j in across_tm:
        crossing_pairs.append((i * slabs + centre_cut - 1, j * slabs + centre_cut))
        crossing_pairs.append((i * slabs + centre_cut, j * slabs + centre_cut - 1))

    arrived_source = lax.ppermute(source, "tm", across_tm)
    arrived = []
    offset = 0
    for count in CHUNKS:
        arrived.append(lax.ppermute(own_initial[offset : offset + count], "tm", across_tm))
        offset += count

    def edge_of(stack):
        return jnp.where(slab_index == centre_cut, stack[:, :HALO], stack[:, layers - HALO :])

    edge = jnp.concatenate([edge_of(a) for a in (source, decay_rate[None], own_initial)], axis=0)
    across = lax.ppermute(edge, ("tm", "slab"), crossing_pairs)

    partner = (tm_index + half_way) % groups
    flags = jnp.stack(
        [
            slab_index > 0,
            slab_index < slabs - 1,
            slab_index == centre_cut,
            slab_index == centre_cut - 1,
        ]
    ).astype(jnp.int32)
    row = lax.dynamic_index_in_dim(release, partner, 0, keepdims=False)
    scalars = jnp.concatenate([row, flags])

    both = jnp.concatenate([arrived_source, decay_rate[None]], axis=0)
    before = lax.ppermute(both, "slab", upward)
    after = lax.ppermute(both, "slab", downward)
    centre, field, matrix = prepare(
        slabs, smooth_taps, arrived_source, decay_rate, before, after
    )

    carried = ()
    offset = 0
    for index, count in enumerate(CHUNKS):
        middle = arrived[index]
        last = index == len(CHUNKS) - 1
        before = lax.ppermute(middle[:, layers - HALO :] if last else middle, "slab", upward)
        after = lax.ppermute(middle[:, :HALO] if last else middle, "slab", downward)
        carried = run_chunk(
            count,
            offset,
            last,
            scalars,
            middle,
            before,
            after,
            across,
            observed,
            centre,
            field,
            carried,
        )
        offset += count

    width = layers + 2 * HALO
    blocks = carried[0].reshape(slabs, width, carried[0].shape[-1])
    columns = lax.all_to_all(blocks, "slab", split_axis=0, concat_axis=0, tiled=True)
    columns = columns.reshape(slabs * width, blocks.shape[-1])
    smoothed = smooth(matrix, columns)
    return (smoothed[0].T[None], smoothed[1].T[None])


def solution(mesh):
    placed = (
        P("tm", None, "slab", None, None),
        P("tm", "slab", None, None),
        P("slab", None, None),
        P("tm", None, "slab", None, None),
        P(),
        P(),
    )

    return jax.shard_map(
        body,
        mesh=mesh,
        in_specs=placed,
        out_specs=(P("tm", None, "slab"), P("tm", None, "slab")),
        check_vma=False,
    )
```

profile of v0, /device:TPU:1, one launch (start us, length us, event | category | flops | bytes accessed | tf_op | source)
XLA Modules:
  0.0 160.9 jit_solution(16561504893945546567)
XLA Ops:
  0.7 8.6 %collective-permute-start = (f32[1,8,16,128]{3,2,1,0:T(8,128)}, f32[1,8,16,128]{3,2,1,0:T(8,128)S(1)}, u32[]{:S(2)}, u32[]{:S(2)}) collective-permute-start(f32[1,8,16,128]{3,2,1,0:T(8,128)} %param.7), channel_id=1, source_target_pairs={{0,384},{32,416},{64,448},{96,480},{128,512},{160,544},{192,576},{... | collective-permute-start | bytes 196616 | tf_op jit(solution)/shard_map/ppermute | solution.py:311
  9.2 1.1 slice_bitcast_fusion
  10.4 2.1 %collective-permute-start.7 = (f32[10,8,16,128]{3,2,1,0:T(8,128)S(1)}, f32[10,8,16,128]{3,2,1,0:T(8,128)S(1)}, u32[]{:S(2)}, u32[]{:S(2)}) collective-permute-start(f32[10,8,16,128]{3,2,1,0:T(8,128)S(1)} %slice_bitcast_fusion), channel_id=1, source_target_pairs={{0,384},{32,416},{64,448},{96,480},{128,512},{160,544},{192,576},{... | collective-permute-start | bytes 1966088 | tf_op jit(solution)/shard_map/ppermute | solution.py:315
  12.5 0.8 slice_bitcast_fusion.1
  13.2 5.1 %collective-permute-start.3 = (f32[6,8,16,128]{3,2,1,0:T(8,128)}, f32[6,8,16,128]{3,2,1,0:T(8,128)S(1)}, u32[]{:S(2)}, u32[]{:S(2)}) collective-permute-start(f32[6,8,16,128]{3,2,1,0:T(8,128)} %slice_bitcast_fusion.1), channel_id=1, source_target_pairs={{0,384},{32,416},{64,448},{96,480},{128,512},{160,544},{192,576},{... | collective-permute-start | bytes 1179656 | tf_op jit(solution)/shard_map/ppermute | solution.py:315
  18.4 0.1 slice_select_fusion
  18.5 0.8 copy-done.7
  19.3 54.0 %collective-permute-done.7.refs_1_ = f32[10,8,16,128]{3,2,1,0:T(8,128)S(1)} collective-permute-done((f32[10,8,16,128]{3,2,1,0:T(8,128)S(1)}, f32[10,8,16,128]{3,2,1,0:T(8,128)S(1)}, u32[]{:S(2)}, u32[]{:S(2)}) %collective-permute-start.7) | collective-permute-done | bytes 655392 | tf_op jit(solution)/shard_map/ppermute | solution.py:315
  73.3 7.5 %collective-permute-start.8 = (f32[10,8,16,128]{3,2,1,0:T(8,128)S(1)}, f32[10,8,16,128]{3,2,1,0:T(8,128)S(1)}, u32[]{:S(2)}, u32[]{:S(2)}) collective-permute-start(f32[10,8,16,128]{3,2,1,0:T(8,128)S(1)} %collective-permute-done.7.refs_1_), channel_id=1, source_target_pairs={{0,1},{1,2},{2,3},{3,4},{4,5},{5,6},{6,7},{7,8},{8,9},{9,10},{10,1... | collective-permute-start | bytes 1966088 | tf_op jit(solution)/shard_map/ppermute | solution.py:348
  80.8 3.1 %collective-permute-start.9 = (f32[10,8,16,128]{3,2,1,0:T(8,128)S(1)}, f32[10,8,16,128]{3,2,1,0:T(8,128)S(1)}, u32[]{:S(2)}, u32[]{:S(2)}) collective-permute-start(f32[10,8,16,128]{3,2,1,0:T(8,128)S(1)} %collective-permute-done.7.refs_1_), channel_id=1, source_target_pairs={{1,0},{2,1},{3,2},{4,3},{5,4},{6,5},{7,6},{8,7},{9,8},{10,9},{11,1... | collective-permute-start | bytes 1966088 | tf_op jit(solution)/shard_map/ppermute | solution.py:349
  83.9 0.9 pad_maximum_fusion
  84.7 0.7 collective-permute-start.6
  85.5 0.2 dynamic-slice_reduce_fusion
  85.7 0.6 copy-done.8
  86.3 2.5 %collective-permute-start.1 = (f32[2,8,16,128]{3,2,1,0:T(8,128)S(1)}, f32[2,8,16,128]{3,2,1,0:T(8,128)S(1)}, u32[]{:S(2)}, u32[]{:S(2)}) collective-permute-start(f32[2,8,16,128]{3,2,1,0:T(8,128)S(1)} %pad_maximum_fusion.1), channel_id=1, source_target_pairs={{0,1},{1,2},{2,3},{3,4},{4,5},{5,6},{6,7},{7,8},{8,9},{9,10},{10,1... | collective-permute-start | bytes 393224 | tf_op jit(solution)/shard_map/ppermute | solution.py:337
  88.8 1.9 %collective-permute-start.2 = (f32[2,8,16,128]{3,2,1,0:T(8,128)S(1)}, f32[2,8,16,128]{3,2,1,0:T(8,128)S(1)}, u32[]{:S(2)}, u32[]{:S(2)}) collective-permute-start(f32[2,8,16,128]{3,2,1,0:T(8,128)S(1)} %pad_maximum_fusion.1), channel_id=1, source_target_pairs={{1,0},{2,1},{3,2},{4,3},{5,4},{6,5},{7,6},{8,7},{9,8},{10,9},{11,1... | collective-permute-start | bytes 393224 | tf_op jit(solution)/shard_map/ppermute | solution.py:338
  90.8 0.8 fusion
  91.6 0.6 copy-done.11
  92.2 3.6 %collective-permute-start.4 = (f32[6,4,16,128]{3,2,1,0:T(8,128)}, f32[6,4,16,128]{3,2,1,0:T(8,128)S(1)}, u32[]{:S(2)}, u32[]{:S(2)}) collective-permute-start(f32[6,4,16,128]{3,2,1,0:T(8,128)} %get-tuple-element.17), channel_id=1, source_target_pairs={{0,1},{1,2},{2,3},{3,4},{4,5},{5,6},{6,7},{7,8},{8,9},{9,10},{10,1... | collective-permute-start | bytes 589832 | tf_op jit(solution)/shard_map/ppermute | solution.py:348
  95.9 1.9 %collective-permute-start.5 = (f32[6,4,16,128]{3,2,1,0:T(8,128)}, f32[6,4,16,128]{3,2,1,0:T(8,128)S(1)}, u32[]{:S(2)}, u32[]{:S(2)}) collective-permute-start(f32[6,4,16,128]{3,2,1,0:T(8,128)} %get-tuple-element.16), channel_id=1, source_target_pairs={{1,0},{2,1},{3,2},{4,3},{5,4},{6,5},{7,6},{8,7},{9,8},{10,9},{11,1... | collective-permute-start | bytes 589832 | tf_op jit(solution)/shard_map/ppermute | solution.py:349
  97.8 0.1 add_convert_fusion
  97.9 0.6 pad_add_fusion.refs_0_
  98.5 3.5 %prepare.1 = (f32[14,16,128]{2,1,0:T(8,128)}, f32[14,16,128]{2,1,0:T(8,128)}, f32[512,256]{1,0:T(8,128)}) custom-call(f32[31]{0:T(128)} %taps.1, f32[1,8,16,128]{3,2,1,0:T(8,128)} %copy-done.8, f32[8,16,128]{2,1,0:T(8,128)} %decay.1, f32[2,8,16,128]{3,2,1,0:T(8,128)} %copy-done.11, f32[2,8,16,128]{3,2,1,0:T(8,128)} %copy-done.12), custom_call_target="tpu_custom_call" | custom-call | flops 8000000 | bytes 2000000 | tf_op jit(solution)/shard_map/prepare/pallas_call | solution.py:255
  102.0 0.8 copy-done.1
  102.7 0.2 copy-done.5
  103.0 0.2 copy-done.6
  103.2 9.8 %chunk.1 = (f32[14,16,128]{2,1,0:T(8,128)}, f32[14,16,128]{2,1,0:T(8,128)}) custom-call(s32[20]{0:T(128)} %pad_add_fusion.refs_0_, f32[10,8,16,128]{3,2,1,0:T(8,128)} %copy-done.4, f32[10,8,16,128]{3,2,1,0:T(8,128)} %copy-done.5, f32[10,8,16,128]{3,2,1,0:T(8,128)} %copy-done.6, f32[18,4,16,128]{3,2,1,0:T(8,128)} %copy-done.1, f32[18,4,16,128]{3,2,1,0:T(8,128)} %copy-done.1, ...), custom_call_target="tpu_custom_call" | custom-call | flops 40000000 | bytes 2500000 | tf_op jit(solution)/shard_map/chunk/pallas_call | solution.py:195
  113.0 0.6 copy-done.9
  113.7 0.1 copy-done.10
  113.8 6.7 %last_chunk.1 = f32[16,2,16,128]{3,2,1,0:T(8,128)} custom-call(s32[20]{0:T(128)} %pad_add_fusion.refs_0_, f32[6,8,16,128]{3,2,1,0:T(8,128)} %copy-done.3, f32[6,4,16,128]{3,2,1,0:T(8,128)} %copy-done.9, f32[6,4,16,128]{3,2,1,0:T(8,128)} %copy-done.10, f32[18,4,16,128]{3,2,1,0:T(8,128)} %copy-done.1, f32[18,4,16,128]{3,2,1,0:T(8,128)} %copy-done.1, ...), custom_call_target="tpu_custom_call" | custom-call | flops 24000000 | bytes 1500000 | tf_op jit(solution)/shard_map/last_chunk/pallas_call | solution.py:195
  120.5 38.2 %all_to_all.5 = f32[32,16,128]{2,1,0:T(8,128)} all-to-all(f32[32,16,128]{2,1,0:T(8,128)} %bitcast.19), channel_id=1, replica_groups=mesh['tm'=24,'slab'=32] {'slab'}, dimensions={0} | all-to-all | bytes 524288 | tf_op jit(solution)/shard_map/all_to_all | solution.py:368
  158.7 2.2 %smooth.1 = (f32[64,256]{1,0:T(8,128)}, f32[64,256]{1,0:T(8,128)}) custom-call(f32[512,256]{1,0:T(8,128)} %get-tuple-element.9.matrix, f32[512,128]{1,0:T(8,128)} %bitcast.20), custom_call_target="tpu_custom_call" | custom-call | tf_op jit(solution)/shard_map/smooth/pallas_call | solution.py:284
  (32 shorter events, 0.1 us)
Async XLA Ops:
  0.6 84.8 %copy-start = (s32[24,16]{0,1:T(8,128)S(1)}, s32[24,16]{0,1:T(8,128)}, u32[]{:S(2)}) copy-start(s32[24,16]{0,1:T(8,128)} %param.10) | copy-start | bytes 4612
  0.6 11.8 %copy-start.2 = (f32[1,16,8,16,128]{4,3,2,1,0:T(8,128)S(1)}, f32[1,16,8,16,128]{4,3,2,1,0:T(8,128)}, u32[]{:S(2)}) copy-start(f32[1,16,8,16,128]{4,3,2,1,0:T(8,128)} %param.6) | copy-start | bytes 3145732
  0.7 85.0 %collective-permute-start = (f32[1,8,16,128]{3,2,1,0:T(8,128)}, f32[1,8,16,128]{3,2,1,0:T(8,128)S(1)}, u32[]{:S(2)}, u32[]{:S(2)}) collective-permute-start(f32[1,8,16,128]{3,2,1,0:T(8,128)} %param.7), channel_id=1, source_target_pairs={{0,384},{32,416},{64,448},{96,480},{128,512},{160,544},{192,576},{... | collective-permute-start | bytes 196616 | tf_op jit(solution)/shard_map/ppermute | solution.py:311
  10.4 8.0 %copy-start.13 = (f32[1,8,16,128]{3,2,1,0:T(8,128)S(1)}, f32[1,8,16,128]{3,2,1,0:T(8,128)}, u32[]{:S(2)}) copy-start(f32[1,8,16,128]{3,2,1,0:T(8,128)} %param.7) | copy-start | bytes 196612
  10.4 62.9 %collective-permute-start.7 = (f32[10,8,16,128]{3,2,1,0:T(8,128)S(1)}, f32[10,8,16,128]{3,2,1,0:T(8,128)S(1)}, u32[]{:S(2)}, u32[]{:S(2)}) collective-permute-start(f32[10,8,16,128]{3,2,1,0:T(8,128)S(1)} %slice_bitcast_fusion), channel_id=1, source_target_pairs={{0,384},{32,416},{64,448},{96,480},{128,512},{160,544},{192,576},{... | collective-permute-start | bytes 1966088 | tf_op jit(solution)/shard_map/ppermute | solution.py:315
  13.2 75.6 %collective-permute-start.3 = (f32[6,8,16,128]{3,2,1,0:T(8,128)}, f32[6,8,16,128]{3,2,1,0:T(8,128)S(1)}, u32[]{:S(2)}, u32[]{:S(2)}) collective-permute-start(f32[6,8,16,128]{3,2,1,0:T(8,128)} %slice_bitcast_fusion.1), channel_id=1, source_target_pairs={{0,384},{32,416},{64,448},{96,480},{128,512},{160,544},{192,576},{... | collective-permute-start | bytes 1179656 | tf_op jit(solution)/shard_map/ppermute | solution.py:315
  18.4 0.8 copy-start.7
  73.3 12.5 %copy-start.4 = (f32[10,8,16,128]{3,2,1,0:T(8,128)}, f32[10,8,16,128]{3,2,1,0:T(8,128)S(1)}, u32[]{:S(2)}) copy-start(f32[10,8,16,128]{3,2,1,0:T(8,128)S(1)} %collective-permute-done.7.refs_1_) | copy-start | bytes 1966084
  73.3 28.7 %collective-permute-start.8 = (f32[10,8,16,128]{3,2,1,0:T(8,128)S(1)}, f32[10,8,16,128]{3,2,1,0:T(8,128)S(1)}, u32[]{:S(2)}, u32[]{:S(2)}) collective-permute-start(f32[10,8,16,128]{3,2,1,0:T(8,128)S(1)} %collective-permute-done.7.refs_1_), channel_id=1, source_target_pairs={{0,1},{1,2},{2,3},{3,4},{4,5},{5,6},{6,7},{7,8},{8,9},{9,10},{10,1... | collective-permute-start | bytes 1966088 | tf_op jit(solution)/shard_map/ppermute | solution.py:348
  80.8 21.1 %collective-permute-start.9 = (f32[10,8,16,128]{3,2,1,0:T(8,128)S(1)}, f32[10,8,16,128]{3,2,1,0:T(8,128)S(1)}, u32[]{:S(2)}, u32[]{:S(2)}) collective-permute-start(f32[10,8,16,128]{3,2,1,0:T(8,128)S(1)} %collective-permute-done.7.refs_1_), channel_id=1, source_target_pairs={{1,0},{2,1},{3,2},{4,3},{5,4},{6,5},{7,6},{8,7},{9,8},{10,9},{11,1... | collective-permute-start | bytes 1966088 | tf_op jit(solution)/shard_map/ppermute | solution.py:349
  84.7 17.2 %collective-permute-start.6 = (f32[18,4,16,128]{3,2,1,0:T(8,128)}, f32[18,4,16,128]{3,2,1,0:T(8,128)S(1)}, u32[]{:S(2)}, u32[]{:S(2)}) collective-permute-start(f32[18,4,16,128]{3,2,1,0:T(8,128)} %pad_maximum_fusion), channel_id=1, source_target_pairs={{15,400},{16,399},{47,432},{48,431},{79,464},{80,463},{111,496},{1... | collective-permute-start | bytes 1769480 | tf_op jit(solution)/shard_map/ppermute | solution.py:322
  85.7 0.6 copy-start.8
  86.3 5.2 %collective-permute-start.1 = (f32[2,8,16,128]{3,2,1,0:T(8,128)S(1)}, f32[2,8,16,128]{3,2,1,0:T(8,128)S(1)}, u32[]{:S(2)}, u32[]{:S(2)}) collective-permute-start(f32[2,8,16,128]{3,2,1,0:T(8,128)S(1)} %pad_maximum_fusion.1), channel_id=1, source_target_pairs={{0,1},{1,2},{2,3},{3,4},{4,5},{5,6},{6,7},{7,8},{8,9},{9,10},{10,1... | collective-permute-start | bytes 393224 | tf_op jit(solution)/shard_map/ppermute | solution.py:337
  88.8 2.7 %copy-start.3 = (f32[6,8,16,128]{3,2,1,0:T(8,128)}, f32[6,8,16,128]{3,2,1,0:T(8,128)S(1)}, u32[]{:S(2)}) copy-start(f32[6,8,16,128]{3,2,1,0:T(8,128)S(1)} %collective-permute-done.3.refs_1_) | copy-start | bytes 1179652
  88.8 7.0 %collective-permute-start.2 = (f32[2,8,16,128]{3,2,1,0:T(8,128)S(1)}, f32[2,8,16,128]{3,2,1,0:T(8,128)S(1)}, u32[]{:S(2)}, u32[]{:S(2)}) collective-permute-start(f32[2,8,16,128]{3,2,1,0:T(8,128)S(1)} %pad_maximum_fusion.1), channel_id=1, source_target_pairs={{1,0},{2,1},{3,2},{4,3},{5,4},{6,5},{7,6},{8,7},{9,8},{10,9},{11,1... | collective-permute-start | bytes 393224 | tf_op jit(solution)/shard_map/ppermute | solution.py:338
  91.5 0.7 copy-start.11
  92.2 20.8 %collective-permute-start.4 = (f32[6,4,16,128]{3,2,1,0:T(8,128)}, f32[6,4,16,128]{3,2,1,0:T(8,128)S(1)}, u32[]{:S(2)}, u32[]{:S(2)}) collective-permute-start(f32[6,4,16,128]{3,2,1,0:T(8,128)} %get-tuple-element.17), channel_id=1, source_target_pairs={{0,1},{1,2},{2,3},{3,4},{4,5},{5,6},{6,7},{7,8},{8,9},{9,10},{10,1... | collective-permute-start | bytes 589832 | tf_op jit(solution)/shard_map/ppermute | solution.py:348
  95.8 2.6 %copy-start.12 = (f32[2,8,16,128]{3,2,1,0:T(8,128)}, f32[2,8,16,128]{3,2,1,0:T(8,128)S(1)}, u32[]{:S(2)}) copy-start(f32[2,8,16,128]{3,2,1,0:T(8,128)S(1)} %collective-permute-done.2.after) | copy-start | bytes 393220
  95.9 17.2 %collective-permute-start.5 = (f32[6,4,16,128]{3,2,1,0:T(8,128)}, f32[6,4,16,128]{3,2,1,0:T(8,128)S(1)}, u32[]{:S(2)}, u32[]{:S(2)}) collective-permute-start(f32[6,4,16,128]{3,2,1,0:T(8,128)} %get-tuple-element.16), channel_id=1, source_target_pairs={{1,0},{2,1},{3,2},{4,3},{5,4},{6,5},{7,6},{8,7},{9,8},{10,9},{11,1... | collective-permute-start | bytes 589832 | tf_op jit(solution)/shard_map/ppermute | solution.py:349
  101.9 0.8 copy-start.1
  101.9 1.0 copy-start.5
  101.9 1.3 copy-start.6
  113.0 0.7 copy-start.9
  113.0 0.7 copy-start.10
where the time goes:
time: 162 us; the launch traced here: 161 us
  waiting for transfers between devices  54 us (33%)
  blocking collectives  38.2 us (24%)
  starting transfers between devices  37 us (23%)
  Pallas kernels  22.2 us (14%)
  local copies, waits for them, and re-layouts  6.91 us (4%)
  other arithmetic  1.63 us (1%)
    ppermute x2, waiting for transfers between devices, body(): lax.ppermute(own_initial[offset:offset + count], 'tm', across_tm)  54 us
    all_to_all x1, blocking collectives, body(): lax.all_to_all(blocks, 'slab', split_axis=0, concat_axis=0, tiled=True)  38.2 us
    pallas_call x2, Pallas kernels, run_chunk(): pl.pallas_call(kernel, grid=(count,), out_shape=shapes, in_specs=[pl.Bloc...  16.5 us
    ppermute x2, starting transfers between devices, body(): lax.ppermute(middle[:, layers - HALO:] if last else middle, 'slab', upward)  11.2 us
    ppermute x1, starting transfers between devices, body(): arrived_source = lax.ppermute(source, 'tm', across_tm)  8.57 us
    ppermute x2, starting transfers between devices, body(): lax.ppermute(own_initial[offset:offset + count], 'tm', across_tm)  7.2 us
    ppermute x2, starting transfers between devices, body(): after = lax.ppermute(middle[:, :HALO] if last else middle, 'slab', downward)  4.98 us
    unnamed x28, local copies, waits for them, and re-layouts  4.01 us
  transfers between devices with their start and end apart: 10, of which 1 were waited for; matrix products, arithmetic and copies ran while one was open for 3% of the time, Pallas kernels for 8%

commit v1 on v0

--- a/solution.py
+++ b/solution.py
@@ -8,7 +8,7 @@
 STEPS = 4
 REACH = STEPS - 1
 HALO = STEPS
-CHUNKS = (10, 6)
+CHUNKS = (11, 5)
 
 vertical_rate = 0.2
 lateral_rate = 0.1
@@ -213,6 +213,7 @@
         cost_estimate=pl.CostEstimate(
             flops=count * 4000000, bytes_accessed=count * 250000, transcendentals=0
         ),
+        compiler_params=pltpu.CompilerParams(vmem_limit_bytes=16 << 20),
         name="last_chunk" if last else "chunk",
     )(scalars, middle, before, after, across, across, observed, centre, field, *carried)
 
@@ -260,6 +261,7 @@
         + [pl.BlockSpec(a.shape, lambda c, n=a.ndim: (0,) * n) for a in (source, decay, before, after)],
         out_specs=tuple(pl.BlockSpec(a.shape, lambda c, n=len(a.shape): (0,) * n) for a in (wide, wide, matrix)),
         cost_estimate=pl.CostEstimate(flops=8000000, bytes_accessed=2000000, transcendentals=0),
+        compiler_params=pltpu.CompilerParams(vmem_limit_bytes=8 << 20),
         name="prepare",
     )(taps, source, decay, before, after)
 
@@ -286,6 +288,7 @@
         out_shape=(shape, shape),
         in_specs=[vmem(), vmem()],
         out_specs=(vmem(), vmem()),
+        compiler_params=pltpu.CompilerParams(vmem_limit_bytes=8 << 20),
         name="smooth",
     )(matrix, columns)
 

time: 162 us -> 155 us (0.957)
  Pallas kernels: 22.2 us -> 16.4 us
    ppermute x1, starting transfers between devices: 8.57 us -> 1.92 us  [body(): arrived_source = lax.ppermute(source, 'tm', across_tm)]
    ppermute x2, starting transfers between devices: 7.2 us -> 13.6 us  [body(): lax.ppermute(own_initial[offset:offset + count], 'tm', across_tm)]
    pallas_call x2, Pallas kernels: 16.5 us -> 13.2 us  [run_chunk(): pl.pallas_call(kernel, grid=(count,), out_shape=shapes, in_specs=[pl.Bloc...]
    unnamed x28 -> x18, local copies, waits for them, and re-layouts: 4.01 us -> 3.69 us
  transfers between devices with their start and end apart: 10 -> 10, of which waited for: 1 -> 1; matrix products, arithmetic and copies ran while one was open for 3% -> 2% of each run, Pallas kernels for 8% -> 7%
where the time goes in v1:
time: 155 us; the launch traced here: 154 us
  waiting for transfers between devices  52.6 us (34%)
  blocking collectives  38.1 us (25%)
  starting transfers between devices  37.1 us (24%)
  Pallas kernels  16.4 us (11%)
  local copies, waits for them, and re-layouts  6.62 us (4%)
  other arithmetic  1.9 us (1%)
    ppermute x2, waiting for transfers between devices, body(): lax.ppermute(own_initial[offset:offset + count], 'tm', across_tm)  52.6 us
    all_to_all x1, blocking collectives, body(): lax.all_to_all(blocks, 'slab', split_axis=0, concat_axis=0, tiled=True)  38.1 us
    ppermute x2, starting transfers between devices, body(): lax.ppermute(own_initial[offset:offset + count], 'tm', across_tm)  13.6 us
    pallas_call x2, Pallas kernels, run_chunk(): pl.pallas_call(kernel, grid=(count,), out_shape=shapes, in_specs=[pl.Bloc...  13.2 us
    ppermute x2, starting transfers between devices, body(): lax.ppermute(middle[:, layers - HALO:] if last else middle, 'slab', upward)  11.5 us
    ppermute x2, starting transfers between devices, body(): after = lax.ppermute(middle[:, :HALO] if last else middle, 'slab', downward)  4.33 us
    unnamed x18, local copies, waits for them, and re-layouts  3.69 us
    ppermute x1, starting transfers between devices, body(): before = lax.ppermute(both, 'slab', upward)  3.14 us
  transfers between devices with their start and end apart: 10, of which 1 were waited for; matrix products, arithmetic and copies ran while one was open for 2% of the time, Pallas kernels for 7%

profile of v1, /device:TPU:1, one launch (start us, length us, event | category | flops | bytes accessed | tf_op | source)
XLA Modules:
  0.0 153.7 jit_solution(5811059747565876472)
XLA Ops:
  0.6 0.0 copy-start
  0.7 1.3 slice_bitcast_fusion
  1.9 8.4 %collective-permute-start.7 = (f32[11,8,16,128]{3,2,1,0:T(8,128)S(1)}, f32[11,8,16,128]{3,2,1,0:T(8,128)S(1)}, u32[]{:S(2)}, u32[]{:S(2)}) collective-permute-start(f32[11,8,16,128]{3,2,1,0:T(8,128)S(1)} %slice_bitcast_fusion), channel_id=1, source_target_pairs={{0,384},{32,416},{64,448},{96,480},{128,512},{160,544},{192,576},{... | collective-permute-start | bytes 2162696 | tf_op jit(solution)/shard_map/ppermute | solution.py:318
  10.4 1.9 %collective-permute-start = (f32[1,8,16,128]{3,2,1,0:T(8,128)}, f32[1,8,16,128]{3,2,1,0:T(8,128)S(1)}, u32[]{:S(2)}, u32[]{:S(2)}) collective-permute-start(f32[1,8,16,128]{3,2,1,0:T(8,128)} %param.7), channel_id=1, source_target_pairs={{0,384},{32,416},{64,448},{96,480},{128,512},{160,544},{192,576},{... | collective-permute-start | bytes 196616 | tf_op jit(solution)/shard_map/ppermute | solution.py:314
  12.3 0.7 slice_bitcast_fusion.1
  13.0 5.1 %collective-permute-start.3 = (f32[5,8,16,128]{3,2,1,0:T(8,128)}, f32[5,8,16,128]{3,2,1,0:T(8,128)S(1)}, u32[]{:S(2)}, u32[]{:S(2)}) collective-permute-start(f32[5,8,16,128]{3,2,1,0:T(8,128)} %slice_bitcast_fusion.1), channel_id=1, source_target_pairs={{0,384},{32,416},{64,448},{96,480},{128,512},{160,544},{192,576},{... | collective-permute-start | bytes 983048 | tf_op jit(solution)/shard_map/ppermute | solution.py:318
  18.2 0.8 slice_select_fusion.2
  19.0 0.1 slice_select_fusion
  19.1 52.6 %collective-permute-done.7.refs_1_ = f32[11,8,16,128]{3,2,1,0:T(8,128)S(1)} collective-permute-done((f32[11,8,16,128]{3,2,1,0:T(8,128)S(1)}, f32[11,8,16,128]{3,2,1,0:T(8,128)S(1)}, u32[]{:S(2)}, u32[]{:S(2)}) %collective-permute-start.7) | collective-permute-done | bytes 720928 | tf_op jit(solution)/shard_map/ppermute | solution.py:318
  71.7 7.4 %collective-permute-start.8 = (f32[11,8,16,128]{3,2,1,0:T(8,128)S(1)}, f32[11,8,16,128]{3,2,1,0:T(8,128)S(1)}, u32[]{:S(2)}, u32[]{:S(2)}) collective-permute-start(f32[11,8,16,128]{3,2,1,0:T(8,128)S(1)} %collective-permute-done.7.refs_1_), channel_id=1, source_target_pairs={{0,1},{1,2},{2,3},{3,4},{4,5},{5,6},{6,7},{7,8},{8,9},{9,10},{10,1... | collective-permute-start | bytes 2162696 | tf_op jit(solution)/shard_map/ppermute | solution.py:351
  79.1 2.4 %collective-permute-start.9 = (f32[11,8,16,128]{3,2,1,0:T(8,128)S(1)}, f32[11,8,16,128]{3,2,1,0:T(8,128)}, u32[]{:S(2)}, u32[]{:S(2)}) collective-permute-start(f32[11,8,16,128]{3,2,1,0:T(8,128)S(1)} %collective-permute-done.7.refs_1_), channel_id=1, source_target_pairs={{1,0},{2,1},{3,2},{4,3},{5,4},{6,5},{7,6},{8,7},{9,8},{10,9},{11,1... | collective-permute-start | bytes 2162696 | tf_op jit(solution)/shard_map/ppermute | solution.py:352
  81.6 0.0 copy-start.1
  81.6 0.9 pad_maximum_fusion
  82.5 0.7 collective-permute-start.6
  83.2 3.1 %collective-permute-start.1 = (f32[2,8,16,128]{3,2,1,0:T(8,128)S(1)}, f32[2,8,16,128]{3,2,1,0:T(8,128)S(1)}, u32[]{:S(2)}, u32[]{:S(2)}) collective-permute-start(f32[2,8,16,128]{3,2,1,0:T(8,128)S(1)} %pad_maximum_fusion.1), channel_id=1, source_target_pairs={{0,1},{1,2},{2,3},{3,4},{4,5},{5,6},{6,7},{7,8},{8,9},{9,10},{10,1... | collective-permute-start | bytes 393224 | tf_op jit(solution)/shard_map/ppermute | solution.py:340
  86.4 1.9 %collective-permute-start.2 = (f32[2,8,16,128]{3,2,1,0:T(8,128)S(1)}, f32[2,8,16,128]{3,2,1,0:T(8,128)S(1)}, u32[]{:S(2)}, u32[]{:S(2)}) collective-permute-start(f32[2,8,16,128]{3,2,1,0:T(8,128)S(1)} %pad_maximum_fusion.1), channel_id=1, source_target_pairs={{1,0},{2,1},{3,2},{4,3},{5,4},{6,5},{7,6},{8,7},{9,8},{10,9},{11,1... | collective-permute-start | bytes 393224 | tf_op jit(solution)/shard_map/ppermute | solution.py:341
  88.3 0.7 fusion
  89.0 0.6 copy-done.3
  89.7 4.1 %collective-permute-start.4 = (f32[5,4,16,128]{3,2,1,0:T(8,128)}, f32[5,4,16,128]{3,2,1,0:T(8,128)}, u32[]{:S(2)}, u32[]{:S(2)}) collective-permute-start(f32[5,4,16,128]{3,2,1,0:T(8,128)} %get-tuple-element.17), channel_id=1, source_target_pairs={{0,1},{1,2},{2,3},{3,4},{4,5},{5,6},{6,7},{7,8},{8,9},{9,10},{10,1... | collective-permute-start | bytes 491528 | tf_op jit(solution)/shard_map/ppermute | solution.py:351
  93.8 0.6 copy-done.5
  94.4 1.9 %collective-permute-start.5 = (f32[5,4,16,128]{3,2,1,0:T(8,128)}, f32[5,4,16,128]{3,2,1,0:T(8,128)}, u32[]{:S(2)}, u32[]{:S(2)}) collective-permute-start(f32[5,4,16,128]{3,2,1,0:T(8,128)} %get-tuple-element.16), channel_id=1, source_target_pairs={{1,0},{2,1},{3,2},{4,3},{5,4},{6,5},{7,6},{8,7},{9,8},{10,9},{11,1... | collective-permute-start | bytes 491528 | tf_op jit(solution)/shard_map/ppermute | solution.py:352
  96.3 0.1 add_convert_fusion
  96.4 0.2 dynamic-slice_reduce_fusion
  96.6 0.1 pad_add_fusion.refs_0_
  96.7 0.6 copy-done.7
  97.3 0.9 copy-done.4
  98.2 0.9 copy-done.6
  99.1 2.1 %prepare.1 = (f32[14,16,128]{2,1,0:T(8,128)S(1)}, f32[14,16,128]{2,1,0:T(8,128)S(1)}, f32[512,256]{1,0:T(8,128)S(1)}) custom-call(f32[31]{0:T(128)S(1)} %copy-done.7, f32[1,8,16,128]{3,2,1,0:T(8,128)S(1)} %collective-permute-done.source, f32[8,16,128]{2,1,0:T(8,128)S(1)} %copy-done.2, f32[2,8,16,128]{3,2,1,0:T(8,128)S(1)} %copy-done.4, ...), custom_call_target="tpu_custom_call" | custom-call | flops 8000000 | bytes 2000000 | tf_op jit(solution)/shard_map/prepare/pallas_call | solution.py:256
  101.2 8.7 %chunk.1 = (f32[14,16,128]{2,1,0:T(8,128)S(1)}, f32[14,16,128]{2,1,0:T(8,128)S(1)}) custom-call(s32[20]{0:T(128)S(1)} %pad_add_fusion.refs_0_, f32[11,8,16,128]{3,2,1,0:T(8,128)S(1)} %collective-permute-done.7.refs_1_, f32[11,8,16,128]{3,2,1,0:T(8,128)S(1)} %collective-permute-done.8.refs_2_, f32[11,8,16,128]{3,2,1,0:T(8,128)} %collective-permute-done.9.refs_3_, ...), custom_call_target="tpu_custom_call" | custom-call | flops 44000000 | bytes 2750000 | tf_op jit(solution)/shard_map/chunk/pallas_call | solution.py:195
  109.9 4.6 %last_chunk.1 = f32[16,2,16,128]{3,2,1,0:T(8,128)S(1)} custom-call(s32[20]{0:T(128)S(1)} %pad_add_fusion.refs_0_, f32[5,8,16,128]{3,2,1,0:T(8,128)S(1)} %collective-permute-done.3.refs_1_, f32[5,4,16,128]{3,2,1,0:T(8,128)} %collective-permute-done.4.refs_2_, f32[5,4,16,128]{3,2,1,0:T(8,128)} %collective-permute-done.5.refs_3_, ...), custom_call_target="tpu_custom_call" | custom-call | flops 20000000 | bytes 1250000 | tf_op jit(solution)/shard_map/last_chunk/pallas_call | solution.py:195
  114.5 38.1 %all_to_all.5 = f32[32,16,128]{2,1,0:T(8,128)S(1)} all-to-all(f32[32,16,128]{2,1,0:T(8,128)S(1)} %bitcast.19), channel_id=1, replica_groups=mesh['tm'=24,'slab'=32] {'slab'}, dimensions={0} | all-to-all | bytes 524288 | tf_op jit(solution)/shard_map/all_to_all | solution.py:371
  152.6 1.1 smooth.1
  (22 shorter events, 0.1 us)
Async XLA Ops:
  0.6 95.8 %copy-start = (s32[24,16]{0,1:T(8,128)S(1)}, s32[24,16]{0,1:T(8,128)}, u32[]{:S(2)}) copy-start(s32[24,16]{0,1:T(8,128)} %param.10) | copy-start | bytes 4612
  0.6 11.7 %copy-start.8 = (f32[1,16,8,16,128]{4,3,2,1,0:T(8,128)S(1)}, f32[1,16,8,16,128]{4,3,2,1,0:T(8,128)}, u32[]{:S(2)}) copy-start(f32[1,16,8,16,128]{4,3,2,1,0:T(8,128)} %param.6) | copy-start | bytes 3145732
  1.9 69.8 %collective-permute-start.7 = (f32[11,8,16,128]{3,2,1,0:T(8,128)S(1)}, f32[11,8,16,128]{3,2,1,0:T(8,128)S(1)}, u32[]{:S(2)}, u32[]{:S(2)}) collective-permute-start(f32[11,8,16,128]{3,2,1,0:T(8,128)S(1)} %slice_bitcast_fusion), channel_id=1, source_target_pairs={{0,384},{32,416},{64,448},{96,480},{128,512},{160,544},{192,576},{... | collective-permute-start | bytes 2162696 | tf_op jit(solution)/shard_map/ppermute | solution.py:318
  10.4 72.8 %collective-permute-start = (f32[1,8,16,128]{3,2,1,0:T(8,128)}, f32[1,8,16,128]{3,2,1,0:T(8,128)S(1)}, u32[]{:S(2)}, u32[]{:S(2)}) collective-permute-start(f32[1,8,16,128]{3,2,1,0:T(8,128)} %param.7), channel_id=1, source_target_pairs={{0,384},{32,416},{64,448},{96,480},{128,512},{160,544},{192,576},{... | collective-permute-start | bytes 196616 | tf_op jit(solution)/shard_map/ppermute | solution.py:314
  13.0 73.3 %collective-permute-start.3 = (f32[5,8,16,128]{3,2,1,0:T(8,128)}, f32[5,8,16,128]{3,2,1,0:T(8,128)S(1)}, u32[]{:S(2)}, u32[]{:S(2)}) collective-permute-start(f32[5,8,16,128]{3,2,1,0:T(8,128)} %slice_bitcast_fusion.1), channel_id=1, source_target_pairs={{0,384},{32,416},{64,448},{96,480},{128,512},{160,544},{192,576},{... | collective-permute-start | bytes 983048 | tf_op jit(solution)/shard_map/ppermute | solution.py:318
  19.0 62.6 %copy-start.2 = (f32[8,16,128]{2,1,0:T(8,128)S(1)}, f32[8,16,128]{2,1,0:T(8,128)}, u32[]{:S(2)}) copy-start(f32[8,16,128]{2,1,0:T(8,128)} %decay.1) | copy-start | bytes 196612
  71.7 29.5 %collective-permute-start.8 = (f32[11,8,16,128]{3,2,1,0:T(8,128)S(1)}, f32[11,8,16,128]{3,2,1,0:T(8,128)S(1)}, u32[]{:S(2)}, u32[]{:S(2)}) collective-permute-start(f32[11,8,16,128]{3,2,1,0:T(8,128)S(1)} %collective-permute-done.7.refs_1_), channel_id=1, source_target_pairs={{0,1},{1,2},{2,3},{3,4},{4,5},{5,6},{6,7},{7,8},{8,9},{9,10},{10,1... | collective-permute-start | bytes 2162696 | tf_op jit(solution)/shard_map/ppermute | solution.py:351
  79.1 22.1 %collective-permute-start.9 = (f32[11,8,16,128]{3,2,1,0:T(8,128)S(1)}, f32[11,8,16,128]{3,2,1,0:T(8,128)}, u32[]{:S(2)}, u32[]{:S(2)}) collective-permute-start(f32[11,8,16,128]{3,2,1,0:T(8,128)S(1)} %collective-permute-done.7.refs_1_), channel_id=1, source_target_pairs={{1,0},{2,1},{3,2},{4,3},{5,4},{6,5},{7,6},{8,7},{9,8},{10,9},{11,1... | collective-permute-start | bytes 2162696 | tf_op jit(solution)/shard_map/ppermute | solution.py:352
  81.6 19.6 %copy-start.1 = (f32[1,16,8,16,128]{4,3,2,1,0:T(8,128)S(1)}, f32[1,16,8,16,128]{4,3,2,1,0:T(8,128)}, u32[]{:S(2)}) copy-start(f32[1,16,8,16,128]{4,3,2,1,0:T(8,128)} %refs_6_.3) | copy-start | bytes 3145732
  82.5 18.7 %collective-permute-start.6 = (f32[18,4,16,128]{3,2,1,0:T(8,128)}, f32[18,4,16,128]{3,2,1,0:T(8,128)S(1)}, u32[]{:S(2)}, u32[]{:S(2)}) collective-permute-start(f32[18,4,16,128]{3,2,1,0:T(8,128)} %pad_maximum_fusion), channel_id=1, source_target_pairs={{15,400},{16,399},{47,432},{48,431},{79,464},{80,463},{111,496},{1... | collective-permute-start | bytes 1769480 | tf_op jit(solution)/shard_map/ppermute | solution.py:325
  83.2 5.8 %collective-permute-start.1 = (f32[2,8,16,128]{3,2,1,0:T(8,128)S(1)}, f32[2,8,16,128]{3,2,1,0:T(8,128)S(1)}, u32[]{:S(2)}, u32[]{:S(2)}) collective-permute-start(f32[2,8,16,128]{3,2,1,0:T(8,128)S(1)} %pad_maximum_fusion.1), channel_id=1, source_target_pairs={{0,1},{1,2},{2,3},{3,4},{4,5},{5,6},{6,7},{7,8},{8,9},{9,10},{10,1... | collective-permute-start | bytes 393224 | tf_op jit(solution)/shard_map/ppermute | solution.py:340
  86.4 7.4 %collective-permute-start.2 = (f32[2,8,16,128]{3,2,1,0:T(8,128)S(1)}, f32[2,8,16,128]{3,2,1,0:T(8,128)S(1)}, u32[]{:S(2)}, u32[]{:S(2)}) collective-permute-start(f32[2,8,16,128]{3,2,1,0:T(8,128)S(1)} %pad_maximum_fusion.1), channel_id=1, source_target_pairs={{1,0},{2,1},{3,2},{4,3},{5,4},{6,5},{7,6},{8,7},{9,8},{10,9},{11,1... | collective-permute-start | bytes 393224 | tf_op jit(solution)/shard_map/ppermute | solution.py:341
  89.0 0.6 copy-start.3
  89.7 20.2 %collective-permute-start.4 = (f32[5,4,16,128]{3,2,1,0:T(8,128)}, f32[5,4,16,128]{3,2,1,0:T(8,128)}, u32[]{:S(2)}, u32[]{:S(2)}) collective-permute-start(f32[5,4,16,128]{3,2,1,0:T(8,128)} %get-tuple-element.17), channel_id=1, source_target_pairs={{0,1},{1,2},{2,3},{3,4},{4,5},{5,6},{6,7},{7,8},{8,9},{9,10},{10,1... | collective-permute-start | bytes 491528 | tf_op jit(solution)/shard_map/ppermute | solution.py:351
  93.8 0.6 copy-start.5
  94.4 15.5 %collective-permute-start.5 = (f32[5,4,16,128]{3,2,1,0:T(8,128)}, f32[5,4,16,128]{3,2,1,0:T(8,128)}, u32[]{:S(2)}, u32[]{:S(2)}) collective-permute-start(f32[5,4,16,128]{3,2,1,0:T(8,128)} %get-tuple-element.16), channel_id=1, source_target_pairs={{1,0},{2,1},{3,2},{4,3},{5,4},{6,5},{7,6},{8,7},{9,8},{10,9},{11,1... | collective-permute-start | bytes 491528 | tf_op jit(solution)/shard_map/ppermute | solution.py:352
  96.6 0.7 copy-start.7
  97.3 0.9 copy-start.4
  98.2 0.9 copy-start.6
